TPU v7x, 32 devices: a whole 2x2x4 slice. The times are simulated.
32 devices in a mesh: rows: 16 (over z, x, core), feat: 2 (over y).
Axes of the slice: x: 2, y: 2, z: 4, core: 2. Of those that a mesh axis runs over, the one named last changes fastest.
Arguments:
- design: bfloat16 [16384, 16384], P('rows', 'feat'), may hold values from -6 to 6
- flags: int32 [16384], P('rows'), may hold values 0 or 1
- scales: float32 [16384], P('rows'), may hold values from 0.3 to 3
- damping: float32 [2, 8192], P('feat', 'rows'), may hold values from 0.2 to 2
- probes: float32 [32, 2, 8192], P(None, 'feat', 'rows'), may hold values from -6 to 6
Outputs:
- solution: float32 [32, 2, 8192], P(None, 'feat', 'rows')
- residual: float32 [32, 2, 8192], P(None, 'feat', 'rows')
All inputs are finite; a program needn't handle non-finite values. No bound on the sum of `flags` on one device may be relied on, other than what follows from the above.
Results may differ from a plain program's by a relative error of at most 0.0073.
Values may be sent and summed in bfloat16 or wider, within the bound.
A program may use at most 64 MiB of HBM per device.

v0:
```python
import jax
import jax.numpy as jnp
from jax import lax
from jax.sharding import PartitionSpec as P

ITERS = 2


def weigh(partial_value, wrow):
    summed = lax.psum(partial_value, "feat")
    return (wrow[None, :] * summed).astype(jnp.bfloat16)


def norms_block(resid):
    return lax.psum(jnp.sum(resid * resid, axis=1), "feat")


def shards(design, flags, scales, damping, probes):
    rows_dev = design.shape[0]
    total_rows = rows_dev * lax.axis_size("rows")
    wrow = flags.astype(jnp.float32) / (scales * scales) / total_rows
    columns = probes.shape[0]
    damp_full, rhs_full = (
        lax.all_gather(damping, "rows", axis=1, tiled=True),
        lax.all_gather(probes, "rows", axis=2, tiled=True),
    )
    damp = damp_full.reshape(-1)
    rhs = rhs_full.reshape(columns, -1)
    solution = jnp.zeros_like(rhs)
    residual = rhs
    direction = rhs
    norm_now = norms_block(residual)
    for step in range(ITERS):
        p_low = direction.astype(jnp.bfloat16)
        partial_value = lax.dot_general(
            p_low, design, (((1,), (1,)), ((), ())), preferred_element_type=jnp.float32
        )
        weighted = weigh(partial_value, wrow)
        term = jnp.dot(weighted, design, preferred_element_type=jnp.float32)
        image = lax.psum(term, "rows") + damp[None, :] * direction
        curve = lax.psum(jnp.sum(direction * image, axis=1), "feat")
        alpha = norm_now / curve
        solution = solution + alpha[:, None] * direction
        residual = residual - alpha[:, None] * image
        norm_next = norms_block(residual)
        direction = residual + (norm_next / norm_now)[:, None] * direction
        norm_now = norm_next
    width = probes.shape[2]
    offset = lax.axis_index("rows") * width
    own_solution = lax.dynamic_slice_in_dim(solution, offset, width, 1)
    own_residual = lax.dynamic_slice_in_dim(residual, offset, width, 1)
    return (own_solution.reshape(probes.shape), own_residual.reshape(probes.shape))


def solution(mesh):
    placed = (P("rows", "feat"), P("rows"), P("rows"), P("feat", "rows"), P(None, "feat", "rows"))
    return jax.shard_map(
        shards,
        mesh=mesh,
        in_specs=placed,
        out_specs=(P(None, "feat", "rows"), P(None, "feat", "rows")),
        check_vma=False,
    )
```

profile of v0, /device:TPU:0, one launch (start us, length us, event | category | flops | bytes accessed | tf_op | source)
XLA Modules:
  0.0 353.4 jit_solution(5223691146667350313)
XLA Ops:
  7.2 0.0 all-gather.2.cloned.1.call-start
  7.2 1.5 copy.7
  8.7 0.0 all-gather.2.cloned.1.call-update
  8.7 0.0 copy-start.3
  8.7 0.0 all-reduce.6.cloned.1.call-start
  8.8 42.6 %all-gather.2.cloned.1.call-done = f32[32,1,8192]{2,0,1:T(8,128)} async-done(((f32[32,1,512]{2,0,1:T(8,128)}), f32[32,1,8192]{2,0,1:T(8,128)}) %all-gather.2.cloned.1.call-update) | async-done | bytes 1048592 | tf_op jit(solution)/shard_map/all_gather | solution.py:25
  51.4 11.9 %fusion.11 = f32[32,1024]{1,0:T(8,128)} fusion(bf16[1024,8192]{1,0:T(8,128)(2,1)} %param.5, f32[32,1,8192]{2,0,1:T(8,128)} %all-gather.2.cloned.1.call-done), kind=kOutput, calls=%fused_computation.25 | convolution fusion | flops 536870912 | bytes 17956864 | tf_op jit(solution)/shard_map/dot_general | solution.py:35
  63.3 0.0 all-reduce.6.cloned.1.call-update
  63.3 0.0 all-reduce.8.cloned.1.call-start
  63.4 20.6 %all-reduce.6.cloned.1.call-done = f32[32,1024]{1,0:T(8,128)} async-done(((f32[32,1024]{1,0:T(8,128)}), f32[32,1024]{1,0:T(8,128)}) %all-reduce.6.cloned.1.call-update) | async-done | bytes 131088 | tf_op jit(solution)/shard_map/psum | solution.py:10
  84.0 9.8 %fusion.4 = f32[32,8192]{1,0:T(8,128)} fusion(bf16[1024,8192]{1,0:T(8,128)(2,1)} %param.5, f32[32,1024]{1,0:T(8,128)} %all-reduce.6.cloned.1.call-done, f32[1024]{0:T(1024)S(1)} %divide_multiply_fusion), kind=kOutput, calls=%fused_computation.14 | convolution fusion | flops 536936448 | bytes 17960960 | tf_op jit(solution)/shard_map/dot_general | solution.py:39
  93.8 0.0 all-reduce.8.cloned.1.call-update
  93.8 0.0 all-reduce.10.cloned.1.call-start
  93.9 21.7 %all_gather.7 = f32[1,8192]{1,0:T(1,128)S(1)} all-gather(f32[1,512]{1,0:T(1,128)S(1)} %copy-done.3), channel_id=1, replica_groups=mesh['rows'=16,'feat'=2] {'rows'}, dimensions={1}, use_global_device_ids=true | all-gather | bytes 34816 | tf_op jit(solution)/shard_map/all_gather | solution.py:24
  115.6 72.3 %all-reduce.8.cloned.1.call-done = f32[32,8192]{1,0:T(8,128)} async-done(((f32[32,8192]{1,0:T(8,128)}), f32[32,8192]{1,0:T(8,128)}) %all-reduce.8.cloned.1.call-update) | async-done | bytes 1048592 | tf_op jit(solution)/shard_map/psum | solution.py:40
  187.9 1.5 multiply_reduce_fusion.2
  189.5 4.9 %all-reduce = (f32[32]{0:T(128)S(1)}, f32[32]{0:T(128)S(1)}) all-reduce(f32[32]{0:T(128)S(1)} %get-tuple-element.3, f32[32]{0:T(128)S(1)} %get-tuple-element.2), channel_id=1, replica_groups=mesh['rows'=16,'feat'=2] {'feat'}, use_global_device_ids=true, to_apply=%region_1.0 | all-reduce | flops 64 | bytes 512 | tf_op jit(solution)/shard_map/psum | solution.py:15
  194.4 1.6 multiply_reduce_fusion.1
  196.0 4.9 %psum.60 = f32[32]{0:T(128)S(1)} all-reduce(f32[32]{0:T(128)S(1)} %get-tuple-element.8), channel_id=1, replica_groups=mesh['rows'=16,'feat'=2] {'feat'}, use_global_device_ids=true, to_apply=%region_7.0 | all-reduce | flops 32 | bytes 256 | tf_op jit(solution)/shard_map/psum | solution.py:15
  200.9 0.2 multiply_add_fusion.1
  201.1 11.5 %fusion = f32[32,1024]{1,0:T(8,128)} fusion(bf16[1024,8192]{1,0:T(8,128)(2,1)} %param.5, f32[32,8192]{1,0:T(8,128)S(1)} %multiply_add_fusion.1), kind=kOutput, calls=%fused_computation.8 | convolution fusion | flops 537133056 | bytes 17956864 | tf_op jit(solution)/shard_map/dot_general | solution.py:35
  212.6 0.0 all-reduce.10.cloned.1.call-update
  212.6 0.2 all-reduce.12.cloned.1.call-start
  212.8 20.6 %all-reduce.10.cloned.1.call-done = f32[32,1024]{1,0:T(8,128)} async-done(((f32[32,1024]{1,0:T(8,128)}), f32[32,1024]{1,0:T(8,128)}) %all-reduce.10.cloned.1.call-update) | async-done | bytes 131088 | tf_op jit(solution)/shard_map/psum | solution.py:10
  233.4 9.9 %fusion.5 = f32[32,8192]{1,0:T(8,128)} fusion(bf16[1024,8192]{1,0:T(8,128)(2,1)} %param.5, f32[32,1024]{1,0:T(8,128)} %all-reduce.10.cloned.1.call-done, f32[1024]{0:T(1024)S(1)} %divide_multiply_fusion), kind=kOutput, calls=%fused_computation.15 | convolution fusion | flops 536936448 | bytes 17960960 | tf_op jit(solution)/shard_map/dot_general | solution.py:39
  243.3 0.0 all-reduce.12.cloned.1.call-update
  243.3 93.8 %all-reduce.12.cloned.1.call-done = f32[32,8192]{1,0:T(8,128)} async-done(((f32[32,8192]{1,0:T(8,128)}), f32[32,8192]{1,0:T(8,128)}) %all-reduce.12.cloned.1.call-update) | async-done | bytes 1048592 | tf_op jit(solution)/shard_map/psum | solution.py:40
  337.1 2.5 multiply_reduce_fusion
  339.6 4.9 %psum.63 = f32[32]{0:T(128)S(1)} all-reduce(f32[32]{0:T(128)S(1)} %get-tuple-element.6), channel_id=1, replica_groups=mesh['rows'=16,'feat'=2] {'feat'}, use_global_device_ids=true, to_apply=%region_11.0 | all-reduce | flops 32 | bytes 256 | tf_op jit(solution)/shard_map/psum | solution.py:41
  344.6 0.9 dynamic-slice_subtract_fusion
  345.5 0.7 reshape.18
  346.2 0.7 reshape.19
  (11 shorter events, 0.0 us)
Async XLA Ops:
  7.2 56.2 %copy-start.2 = (s32[1024]{0:T(1024)S(1)}, s32[1024]{0:T(1024)}, u32[]{:S(2)}) copy-start(s32[1024]{0:T(1024)} %param.6) | copy-start | bytes 12292
  7.2 56.2 %copy-start.1 = (f32[1024]{0:T(1024)S(1)}, f32[1024]{0:T(1024)}, u32[]{:S(2)}) copy-start(f32[1024]{0:T(1024)} %param.7) | copy-start | bytes 12292
  7.2 44.2 %all-gather.2.cloned.1.call-start = ((), (), s32[]{:S(2)}) async-start(), calls=%async_computation | async-start | bytes 1114112 | tf_op jit(solution)/shard_map/all_gather | solution.py:25
  8.7 85.1 %copy-start.3 = (f32[1,512]{1,0:T(1,128)S(1)}, f32[1,512]{1,0:T(1,128)}, u32[]{:S(2)}) copy-start(f32[1,512]{1,0:T(1,128)} %param.8) | copy-start | bytes 6148
  8.7 75.2 %all-reduce.6.cloned.1.call-start = ((), (), s32[]{:S(2)}) async-start(), calls=%async_computation.1 | async-start | bytes 262144 | tf_op jit(solution)/shard_map/psum | solution.py:10
  51.4 136.5 %copy-start = (f32[32,1,8192]{2,0,1:T(8,128)S(1)}, f32[32,1,8192]{2,0,1:T(8,128)}, u32[]{:S(2)}) copy-start(f32[32,1,8192]{2,0,1:T(8,128)} %all-gather.2.cloned.1.call-done) | copy-start | bytes 3145732
  63.3 124.6 %all-reduce.8.cloned.1.call-start = ((), (), s32[]{:S(2)}) async-start(), calls=%async_computation.2 | async-start | bytes 2097152 | tf_op jit(solution)/shard_map/psum | solution.py:40
  93.8 139.6 %all-reduce.10.cloned.1.call-start = ((), (), s32[]{:S(2)}) async-start(), calls=%async_computation.3 | async-start | bytes 262144 | tf_op jit(solution)/shard_map/psum | solution.py:10
  212.6 124.5 %all-reduce.12.cloned.1.call-start = ((), (), s32[]{:S(2)}) async-start(), calls=%async_computation.4 | async-start | bytes 2097152 | tf_op jit(solution)/shard_map/psum | solution.py:40
Sparse Core Ops, SparseCore 0:
  10.8 40.5 all-gather.1
  63.4 20.5 all-reduce.5
  93.9 93.9 all-reduce.7
  212.7 20.6 all-reduce.9
  243.4 93.6 all-reduce.11
where the time goes:
time: 354 us; the launch traced here: 353 us
  waiting for transfers between devices  250 us (71%)
  matrix products  43 us (12%)
  blocking collectives  36.5 us (10%)
  between operations  13.9 us (4%)
  other arithmetic  6.75 us (2%)
    psum x2, waiting for transfers between devices, shards(): image = lax.psum(term, 'rows') + damp[None, :] * direction  166 us
    all_gather x1, waiting for transfers between devices, shards(): lax.all_gather(probes, 'rows', axis=2, tiled=True)  42.6 us
    psum x2, waiting for transfers between devices, weigh(): summed = lax.psum(partial_value, 'feat')  41.2 us
    dot_general x2, matrix products, shards(): lax.dot_general(p_low, design, (((1,), (1,)), ((), ())), preferred_elemen...  23.4 us
    all_gather x1, blocking collectives, shards(): lax.all_gather(damping, 'rows', axis=1, tiled=True)  21.7 us
    dot_general x2, matrix products, shards(): term = jnp.dot(weighted, design, preferred_element_type=jnp.float32)  19.7 us
    psum x2, blocking collectives, norms_block(): return lax.psum(jnp.sum(resid * resid, axis=1), 'feat')  9.86 us
  transfers between devices with their start and end apart: 5, of which 5 were waited for; matrix products, arithmetic and copies ran while one was open for 0% of the time, Pallas kernels for 0%

commit v1 on v0

--- a/solution.py
+++ b/solution.py
@@ -37,7 +37,7 @@
         )
         weighted = weigh(partial_value, wrow)
         term = jnp.dot(weighted, design, preferred_element_type=jnp.float32)
-        image = lax.psum(term, "rows") + damp[None, :] * direction
+        image = jnp.sum(lax.all_gather(term, "rows"), axis=0) + damp[None, :] * direction
         curve = lax.psum(jnp.sum(direction * image, axis=1), "feat")
         alpha = norm_now / curve
         solution = solution + alpha[:, None] * direction

time: 354 us -> 428 us (1.21)
  waiting for transfers between devices: 250 us -> 313 us
  other arithmetic: 6.75 us -> 17.9 us
    all_gather x0 -> x2, waiting for transfers between devices: none -> 229 us  [shards(): lax.all_gather(term, 'rows')]
    psum x2 -> x0, waiting for transfers between devices: 166 us -> none  [shards(): image = lax.psum(term, 'rows') + damp[None, :] * direction]
    reduce_sum x0 -> x2, other arithmetic: none -> 13.3 us  [shards(): jnp.sum(lax.all_gather(term, 'rows'), axis=0) + damp[None, :] * direction]
where the time goes in v1:
time: 428 us
  waiting for transfers between devices  313 us (73%)
  matrix products  43 us (10%)
  blocking collectives  37 us (9%)
  other arithmetic  17.9 us (4%)
  between operations  13.9 us (3%)
    all_gather x2, waiting for transfers between devices, shards(): lax.all_gather(term, 'rows')  229 us
    all_gather x1, waiting for transfers between devices, shards(): lax.all_gather(probes, 'rows', axis=2, tiled=True)  41.6 us
    psum x2, waiting for transfers between devices, weigh(): summed = lax.psum(partial_value, 'feat')  41 us
    dot_general x2, matrix products, shards(): lax.dot_general(p_low, design, (((1,), (1,)), ((), ())), preferred_elemen...  23.3 us
    all_gather x1, blocking collectives, shards(): lax.all_gather(damping, 'rows', axis=1, tiled=True)  22.1 us
    dot_general x2, matrix products, shards(): term = jnp.dot(weighted, design, preferred_element_type=jnp.float32)  19.7 us
    reduce_sum x2, other arithmetic, shards(): jnp.sum(lax.all_gather(term, 'rows'), axis=0) + damp[None, :] * direction  13.3 us
    psum x2, blocking collectives, norms_block(): return lax.psum(jnp.sum(resid * resid, axis=1), 'feat')  10 us
  transfers between devices with their start and end apart: 5, of which 5 were waited for; matrix products, arithmetic and copies ran while one was open for 0% of the time, Pallas kernels for 0%

profile of v1, /device:TPU:0, one launch (start us, length us, event | category | flops | bytes accessed | tf_op | source)
XLA Modules:
  0.0 427.7 jit_solution(2980783711545165655)
XLA Ops:
  7.2 0.0 all-gather.6.cloned.1.call-start
  7.2 0.7 all-gather.6.cloned.1.call-update
  7.9 0.0 all-reduce.4.cloned.1.call-start
  8.0 41.6 %all-gather.6.cloned.1.call-done = f32[32,1,8192]{2,1,0:T(1,128)} async-done(((f32[32,1,512]{2,1,0:T(1,128)}), f32[32,1,8192]{2,1,0:T(1,128)}) %all-gather.6.cloned.1.call-update) | async-done | bytes 1048592 | tf_op jit(solution)/shard_map/all_gather | solution.py:25
  49.6 11.8 %fusion.2 = f32[32,1024]{1,0:T(8,128)} fusion(bf16[1024,8192]{1,0:T(8,128)(2,1)} %param.5, f32[32,1,8192]{2,1,0:T(1,128)} %all-gather.6.cloned.1.call-done), kind=kOutput, calls=%fused_computation.11 | convolution fusion | flops 536870912 | bytes 17956864 | tf_op jit(solution)/shard_map/dot_general | solution.py:35
  61.4 0.0 all-reduce.4.cloned.1.call-update
  61.4 0.0 all-gather.8.cloned.1.call-start
  61.5 21.2 %all-reduce.4.cloned.1.call-done = f32[32,1024]{1,0:T(8,128)} async-done(((f32[32,1024]{1,0:T(8,128)}), f32[32,1024]{1,0:T(8,128)}) %all-reduce.4.cloned.1.call-update) | async-done | bytes 131088 | tf_op jit(solution)/shard_map/psum | solution.py:10
  82.7 9.9 %fusion.4 = f32[32,8192]{1,0:T(8,128)} fusion(bf16[1024,8192]{1,0:T(8,128)(2,1)} %param.5, f32[32,1024]{1,0:T(8,128)} %all-reduce.4.cloned.1.call-done, f32[1024]{0:T(1024)S(1)} %divide_multiply_fusion), kind=kOutput, calls=%fused_computation.15 | convolution fusion | flops 536936448 | bytes 17960960 | tf_op jit(solution)/shard_map/dot_general | solution.py:39
  92.6 0.0 all-gather.8.cloned.1.call-update
  92.6 0.0 all-reduce.6.cloned.1.call-start
  92.7 22.1 %all_gather.21 = f32[1,8192]{1,0:T(1,128)S(1)} all-gather(f32[1,512]{1,0:T(1,128)S(1)} %copy-done.3), channel_id=1, replica_groups=mesh['rows'=16,'feat'=2] {'rows'}, dimensions={1}, use_global_device_ids=true | all-gather | bytes 34816 | tf_op jit(solution)/shard_map/all_gather | solution.py:24
  114.7 104.5 %all-gather.8.cloned.1.call-done = f32[512,8192]{1,0:T(8,128)} async-done(((f32[32,8192]{1,0:T(8,128)}), f32[512,8192]{1,0:T(8,128)}) %all-gather.8.cloned.1.call-update) | async-done | bytes 16777232 | tf_op jit(solution)/shard_map/all_gather | solution.py:40
  219.2 6.7 %reduce_sum.55 = f32[32,8192]{1,0:T(8,128)S(1)} reduce(f32[16,32,8192]{2,1,0:T(8,128)} %bitcast.23, f32[]{:T(128)} %constant.3.clone.1), dimensions={0}, to_apply=%region_3.0 | reduce | flops 3932160 | bytes 17825796 | tf_op jit(solution)/shard_map/reduce_sum | solution.py:40
  225.9 0.8 multiply_reduce_fusion.2
  226.7 4.9 %all-reduce = (f32[32]{0:T(128)S(1)}, f32[32]{0:T(128)S(1)}) all-reduce(f32[32]{0:T(128)S(1)} %get-tuple-element.3, f32[32]{0:T(128)S(1)} %get-tuple-element.2), channel_id=1, replica_groups=mesh['rows'=16,'feat'=2] {'feat'}, use_global_device_ids=true, to_apply=%region_1.0 | all-reduce | flops 64 | bytes 512 | tf_op jit(solution)/shard_map/psum | solution.py:15
  231.6 0.8 multiply_reduce_fusion.1
  232.5 5.1 %psum.45 = f32[32]{0:T(128)S(1)} all-reduce(f32[32]{0:T(128)S(1)} %get-tuple-element.8), channel_id=1, replica_groups=mesh['rows'=16,'feat'=2] {'feat'}, use_global_device_ids=true, to_apply=%region_7.0 | all-reduce | flops 32 | bytes 256 | tf_op jit(solution)/shard_map/psum | solution.py:15
  237.6 0.7 multiply_add_fusion.1
  238.3 11.5 %fusion = f32[32,1024]{1,0:T(8,128)} fusion(bf16[1024,8192]{1,0:T(8,128)(2,1)} %param.5, f32[32,8192]{1,0:T(8,128)S(1)} %multiply_add_fusion.1), kind=kOutput, calls=%fused_computation.9 | convolution fusion | flops 537133056 | bytes 17956864 | tf_op jit(solution)/shard_map/dot_general | solution.py:35
  249.7 0.0 all-reduce.6.cloned.1.call-update
  249.8 0.0 all-gather.10.cloned.1.call-start
  249.8 19.8 %all-reduce.6.cloned.1.call-done = f32[32,1024]{1,0:T(8,128)} async-done(((f32[32,1024]{1,0:T(8,128)}), f32[32,1024]{1,0:T(8,128)}) %all-reduce.6.cloned.1.call-update) | async-done | bytes 131088 | tf_op jit(solution)/shard_map/psum | solution.py:10
  269.6 9.8 %fusion.5 = f32[32,8192]{1,0:T(8,128)} fusion(bf16[1024,8192]{1,0:T(8,128)(2,1)} %param.5, f32[32,1024]{1,0:T(8,128)} %all-reduce.6.cloned.1.call-done, f32[1024]{0:T(1024)S(1)} %divide_multiply_fusion), kind=kOutput, calls=%fused_computation.16 | convolution fusion | flops 536936448 | bytes 17960960 | tf_op jit(solution)/shard_map/dot_general | solution.py:39
  279.5 1.6 copy.21
  281.1 124.9 %all-gather.10.cloned.1.call-done = f32[512,8192]{1,0:T(8,128)} async-done(((f32[32,8192]{1,0:T(8,128)}), f32[512,8192]{1,0:T(8,128)}) %all-gather.10.cloned.1.call-update) | async-done | bytes 16777232 | tf_op jit(solution)/shard_map/all_gather | solution.py:40
  406.1 6.7 %reduce_sum.58 = f32[32,8192]{1,0:T(8,128)S(1)} reduce(f32[16,32,8192]{2,1,0:T(8,128)} %bitcast.22, f32[]{:T(128)} %constant.3.clone.1), dimensions={0}, to_apply=%region_9.0 | reduce | flops 3932160 | bytes 17825796 | tf_op jit(solution)/shard_map/reduce_sum | solution.py:40
  412.7 1.2 multiply_reduce_fusion
  414.0 4.9 %psum.47 = f32[32]{0:T(128)S(1)} all-reduce(f32[32]{0:T(128)S(1)} %get-tuple-element.6), channel_id=1, replica_groups=mesh['rows'=16,'feat'=2] {'feat'}, use_global_device_ids=true, to_apply=%region_11.0 | all-reduce | flops 32 | bytes 256 | tf_op jit(solution)/shard_map/psum | solution.py:41
  418.9 1.0 dynamic-slice_subtract_fusion
  419.9 0.7 reshape.18
  420.5 0.7 reshape.19
  (13 shorter events, 0.1 us)
Async XLA Ops:
  7.2 54.3 %copy-start.2 = (s32[1024]{0:T(1024)S(1)}, s32[1024]{0:T(1024)}, u32[]{:S(2)}) copy-start(s32[1024]{0:T(1024)} %param.6) | copy-start | bytes 12292
  7.2 54.3 %copy-start.1 = (f32[1024]{0:T(1024)S(1)}, f32[1024]{0:T(1024)}, u32[]{:S(2)}) copy-start(f32[1024]{0:T(1024)} %param.7) | copy-start | bytes 12292
  7.2 42.4 %all-gather.6.cloned.1.call-start = ((), (), s32[]{:S(2)}) async-start(), calls=%async_computation | async-start | bytes 1114112 | tf_op jit(solution)/shard_map/all_gather | solution.py:25
  7.9 84.7 %copy-start.3 = (f32[1,512]{1,0:T(1,128)S(1)}, f32[1,512]{1,0:T(1,128)}, u32[]{:S(2)}) copy-start(f32[1,512]{1,0:T(1,128)} %param.8) | copy-start | bytes 6148
  7.9 74.8 %all-reduce.4.cloned.1.call-start = ((), (), s32[]{:S(2)}) async-start(), calls=%async_computation.1 | async-start | bytes 262144 | tf_op jit(solution)/shard_map/psum | solution.py:10
  61.4 157.8 %all-gather.8.cloned.1.call-start = ((), (), s32[]{:S(2)}) async-start(), calls=%async_computation.3 | async-start | bytes 17825792 | tf_op jit(solution)/shard_map/all_gather | solution.py:40
  61.5 164.4 %copy-start = (f32[32,1,8192]{2,1,0:T(1,128)S(1)}, f32[32,1,8192]{2,1,0:T(1,128)}, u32[]{:S(2)}) copy-start(f32[32,1,8192]{2,1,0:T(1,128)} %all-gather.6.cloned.1.call-done) | copy-start | bytes 3145732
  92.6 177.0 %all-reduce.6.cloned.1.call-start = ((), (), s32[]{:S(2)}) async-start(), calls=%async_computation.2 | async-start | bytes 262144 | tf_op jit(solution)/shard_map/psum | solution.py:10
  249.8 156.3 %all-gather.10.cloned.1.call-start = ((), (), s32[]{:S(2)}) async-start(), calls=%async_computation.4 | async-start | bytes 17825792 | tf_op jit(solution)/shard_map/all_gather | solution.py:40
Sparse Core Ops, SparseCore 0:
  10.1 39.3 all-gather.5
  61.5 21.1 all-reduce.3
  92.7 126.4 all-gather.7
  249.9 19.6 all-reduce.5
  279.6 126.4 all-gather.9
